TPU v7x, 256 devices: a whole 4x4x8 slice. The times are simulated.
256 devices in a mesh: img: 32 (over y, z), ori: 8 (over x, core).
Axes of the slice: x: 4, y: 4, z: 8, core: 2. Of those that a mesh axis runs over, the one named last changes fastest.
Arguments:
- images: bfloat16 [1024, 2, 16256], P('img'), may hold values from -6 to 6
- shifts: int32 [1024], P('img'), may hold values from 0 to 35
- inv_temp: float32 [1024], P('img'), may hold values from 0.5 to 4
- candidates: int32 [32, 512], P('img'), may hold values from 0 to 1023
- volume: bfloat16 [64, 2, 16256], P(None, None, 'img'), may hold values from -6 to 6
- tilts: bfloat16 [1024, 64], P('ori'), may hold values from -1 to 1
- azimuth: float32 [1024], P('ori'), may hold values from -3.140625 to 3.140625
Outputs:
- posteriors: float32 [1024, 1024], P('img', 'ori')
- weighted_sums: float32 [16256, 2, 1024], P('img', None, 'ori')
- volume_grad: float32 [64, 2, 16256], P(None, None, 'img')
Inputs may be any that keep to these rules, and one draw needn't show every extreme that they name: `candidates`: A group's list may name an orientation more than once.
All inputs are finite; a program needn't handle non-finite values.
Results may differ from a plain program's by a relative error of at most 0.017.
Values may be sent and summed in bfloat16 or wider, within the bound.
No kernel may reach another device: no remote copies, remote signals or barrier semaphores. Data moves between devices by JAX's collectives and lax.ppermute only.
A program may use at most 128 MiB of HBM per device.

v0:
```python
import math
import jax
import jax.numpy as jnp
from jax import lax
from jax.sharding import Mesh
from jax.sharding import PartitionSpec as P

NSHIFT = 36
IMG = ("img_0", "img_1")
noise_var = 128.0
masked_fill = -1e30


def sent_to_all(x, axis):
    devices = lax.axis_size(axis)
    return lax.all_to_all(jnp.broadcast_to(x[None], (devices, *x.shape)), axis, 0, 0, tiled=True)


def of_everyone(x, axis):
    return sent_to_all(x, axis).max(axis=0)


def of_everyone_2(x, axis):
    everything = sent_to_all(x, axis)
    return jnp.sum(everything, axis=0)


def split_up(x, dim, devices):
    before, after = (x.shape[:dim], x.shape[dim + 1 :])
    return jnp.moveaxis(x.reshape(*before, devices, -1, *after), dim, 0)


def cut_rows(length, count):
    unit = 8 if length >= 8 * count else 1
    return [length // unit * k // count * unit for k in range(1, count)]


def own_block(tiles, axes, turns):
    inside = tiles.shape[1:]
    tiles = tiles.reshape(*(lax.axis_size(a) for a in axes), *inside)
    tiles = jnp.moveaxis(tiles, turns, range(len(axes))).reshape(-1, *inside)
    for k in turns:
        tiles = lax.psum_scatter(tiles, axes[k], scatter_dimension=0, tiled=True)
    return tiles[0]


def sum_at_once(x, axes, dim):
    tiles = split_up(x, dim, lax.axis_size(axes))
    widest = max(range(1, max(2, tiles.ndim - 1)), key=lambda d: tiles.shape[d])
    count, gathered = (len(axes), [])
    for first, share in enumerate(
        jnp.split(tiles, cut_rows(tiles.shape[widest], count), axis=widest)
    ):
        if share.size:
            turns = [(first + k) % count for k in range(count)]
            gathered.append(own_block(share, axes, turns))
    return jnp.concatenate(gathered, axis=widest - 1)


def over_copies(x, axis):
    everything = sent_to_all(x, axis)
    return jnp.sum(everything.astype(jnp.float32), axis=0)


def order_table(start, width):
    return ((start + jnp.arange(width, dtype=jnp.int32)) % 64 - 32).astype(jnp.float32)


def project_piece(piece, start, tilts, azimuth):
    width = piece.shape[2]
    degrees = piece.shape[0]
    mixed = jnp.dot(tilts, piece.reshape(degrees, 2 * width), preferred_element_type=jnp.float32)
    mixed = mixed.reshape(tilts.shape[0], 2, width)
    angles = azimuth[:, None] * order_table(start, width)[None, :]
    cosine = jnp.cos(angles)
    sine = jnp.sin(angles)
    real_part = mixed[:, 0] * cosine - mixed[:, 1] * sine
    imag_part = mixed[:, 0] * sine + mixed[:, 1] * cosine
    return jnp.stack([real_part, imag_part], axis=1).astype(jnp.bfloat16)


def rotate_images(images, shifts):
    width = images.shape[2]
    phase = shifts.astype(jnp.float32) * (2.0 * math.pi / NSHIFT)
    angles = phase[:, None] * order_table(0, width)[None, :]
    cosine = jnp.cos(angles)
    sine = jnp.sin(angles)
    first = images[:, 0].astype(jnp.float32)
    second = images[:, 1].astype(jnp.float32)
    real_part = first * cosine - second * sine
    imag_part = first * sine + second * cosine
    return jnp.stack([real_part, imag_part], axis=1).astype(jnp.bfloat16)


def shards(images, shifts, inv_temp, candidates, volume, tilts, azimuth):
    local_orients = tilts.shape[0]
    part_width = volume.shape[2]
    full_width = images.shape[2]
    image_count = images.shape[0]
    column_start = lax.axis_index(IMG) * part_width
    orient_ids = lax.axis_index("ori") * local_orients + jnp.arange(local_orients, dtype=jnp.int32)
    own_part = project_piece(volume, column_start, tilts, azimuth)
    slices = lax.all_gather(own_part, IMG, axis=2, tiled=True)
    rotated = rotate_images(images, shifts)
    flat_images = rotated.reshape(image_count, 2 * full_width)
    flat_slices = slices.reshape(local_orients, 2 * full_width)
    inner = lax.dot_general(
        flat_images, flat_slices, (((1,), (1,)), ((), ())), preferred_element_type=jnp.float32
    )
    energies = jnp.sum(jnp.square(slices.astype(jnp.float32)), axis=(1, 2))
    scores = inv_temp[:, None] * (inner - 0.5 * energies[None, :]) / noise_var
    allowed = jnp.any(candidates[0][:, None] == orient_ids[None, :], axis=0)
    allowed_rows = jnp.broadcast_to(allowed[None, :], scores.shape)
    held = jnp.where(allowed_rows, scores, masked_fill)
    local_peak = jnp.max(held, axis=1)
    peak = of_everyone(local_peak, "ori")
    local_total = jnp.sum(jnp.where(allowed_rows, jnp.exp(held - peak[:, None]), 0.0), axis=1)
    total = of_everyone_2(local_total, "ori")
    posteriors = jnp.where(allowed_rows, jnp.exp(held - peak[:, None]), 0.0) / total[:, None]
    post_bf = posteriors.astype(jnp.bfloat16)
    mass = of_everyone_2(jnp.sum(posteriors, axis=0), IMG)
    sums = sum_at_once(
        jnp.einsum("ick,io->kco", rotated, post_bf, preferred_element_type=jnp.float32).astype(
            jnp.bfloat16
        ),
        IMG,
        0,
    ).astype(jnp.float32)
    own_slices = lax.dynamic_slice_in_dim(slices, column_start, part_width, 2)
    own = jnp.transpose(own_slices.astype(jnp.float32), (2, 1, 0))
    resid = sums - mass[None, None, :] * own
    angles = order_table(column_start, part_width)[:, None] * azimuth[None, :]
    cosine = jnp.cos(angles)
    sine = jnp.sin(angles)
    back_real = resid[:, 0] * cosine + resid[:, 1] * sine
    back_imag = resid[:, 1] * cosine - resid[:, 0] * sine
    back = jnp.stack([back_real, back_imag], axis=1)
    partial_grad = (
        jnp.einsum("kco,ol->lck", back, tilts.astype(jnp.float32), precision=lax.Precision.HIGHEST)
        / noise_var
    )
    volume_grad = over_copies(partial_grad.astype(jnp.bfloat16), "ori").astype(jnp.float32)
    return (posteriors, sums, volume_grad)


def solution(mesh):
    finer = Mesh(mesh.devices.reshape(4, 8, mesh.shape["ori"]), ("img_0", "img_1", "ori"))
    return jax.shard_map(
        shards,
        mesh=finer,
        in_specs=(
            P(IMG, None, None),
            P(IMG),
            P(IMG),
            P(IMG, None),
            P(None, None, IMG),
            P("ori", None),
            P("ori"),
        ),
        out_specs=(P(IMG, "ori"), P(IMG, None, "ori"), P(None, None, IMG)),
        check_vma=False,
    )
```

profile of v0, /device:TPU:1, one launch (start us, length us, event | category | flops | bytes accessed | tf_op | source)
XLA Modules:
  0.0 394.1 jit_solution(1204516911856662296)
XLA Ops:
  7.3 1.2 reshape.337
  8.9 1.8 fusion.42
  10.8 0.9 copy.50
  11.9 3.0 fusion.66
  14.9 8.0 %fusion.8 = (bf16[32,1,16256]{2,0,1:T(8,128)(2,1)S(1)}, bf16[32,1,16256]{2,0,1:T(8,128)(2,1)S(1)}) fusion(f32[16256]{0:T(1024)S(1)} %fusion.48, f32[32]{0:T(128)S(1)} %convert_multiply_fusion, bf16[32,1,16256]{2,1,0:T(2,128)(2,1)S(1)} %get-tuple-element.23, bf16[32,1,16256]{2,1,0:T(2,128)(2,1)S(1)} %get-tuple-element.22), kind=kLoop, calls=%fused_computation.14 | loop fusion | flops 5722112 | bytes 4226688 | tf_op jit(solution)/shard_map/convert.2
  22.9 89.6 %all-gather.2.cloned.1.call-done = bf16[128,2,16256]{0,1,2:T(2,128)(2,1)} async-done(((bf16[128,2,508]{0,1,2:T(2,128)(2,1)}), bf16[128,2,16256]{0,1,2:T(2,128)(2,1)}) %all-gather.2.cloned.1.call-update) | async-done | bytes 8323088 | tf_op jit(solution)/shard_map/all_gather | solution.py:103
  112.5 18.5 %multiply_reduce_fusion = f32[128]{0:T(128)S(1)} fusion(bf16[128,2,16256]{0,1,2:T(2,128)(2,1)} %all-gather.2.cloned.1.call-done), kind=kLoop, calls=%fused_computation.2 | loop fusion | flops 12484480 | bytes 8323584 | tf_op jit(solution)/shard_map/reduce_sum | solution.py:110
  131.0 1.5 fusion.67
  132.5 10.1 %all_to_all.23 = f32[8,1,32]{2,1,0:T(1,128)S(1)} all-to-all(f32[8,1,32]{2,1,0:T(1,128)S(1)} %broadcast_in_dim.20), channel_id=1, replica_groups=mesh['img_0'=4,'img_1'=8,'ori'=8] {'ori'}, dimensions={0} | all-to-all | bytes 2048 | tf_op jit(solution)/shard_map/all_to_all | solution.py:16
  142.8 7.7 %all_to_all.24 = f32[8,1,32]{2,1,0:T(1,128)S(1)} all-to-all(f32[8,1,32]{2,1,0:T(1,128)S(1)} %broadcast_in_dim.22), channel_id=1, replica_groups=mesh['img_0'=4,'img_1'=8,'ori'=8] {'ori'}, dimensions={0} | all-to-all | bytes 2048 | tf_op jit(solution)/shard_map/all_to_all | solution.py:16
  150.6 5.5 %fusion = bf16[16256,2,128]{0,2,1:T(8,128)(2,1)} fusion(bf16[32,1,16256]{2,0,1:T(8,128)(2,1)S(1)} %get-tuple-element.21, bf16[32,1,16256]{2,0,1:T(8,128)(2,1)S(1)} %get-tuple-element.20, f32[32,128]{1,0:T(8,128)S(1)} %get-tuple-element.19), kind=kOutput, calls=%fused_computation.1 | convolution fusion | flops 274665472 | bytes 10420224 | tf_op jit(solution)/shard_map/ick,io->kco/dot_general | solution.py:123
  156.1 20.1 %reshape.344 = bf16[32,508,2,128]{1,0,3,2:T(8,128)(2,1)} reshape(bf16[16256,2,128]{0,2,1:T(8,128)(2,1)} %fusion) | data formatting | bytes 16646144 | tf_op jit(solution)/shard_map/reshape | solution.py:30
  176.2 9.1 %slice_bitcast_fusion = bf16[4,8,260,2,128]{2,1,0,4,3:T(8,128)(2,1)} fusion(bf16[32,508,2,128]{1,0,3,2:T(8,128)(2,1)} %reshape.344), kind=kLoop, calls=%fused_computation.5 | loop fusion | bytes 8519680 | tf_op jit(solution)/shard_map/reshape | solution.py:40
  185.2 8.4 %copy.56 = bf16[4,8,260,2,128]{4,2,3,0,1:T(8,128)(2,1)} copy(bf16[4,8,260,2,128]{2,1,0,4,3:T(8,128)(2,1)} %slice_bitcast_fusion) | data formatting | bytes 8519680 | tf_op jit(solution)/shard_map/reshape | solution.py:40
  193.7 4.6 %split.8 = bf16[32,248,2,128]{1,0,3,2:T(8,128)(2,1)} slice(bf16[32,508,2,128]{1,0,3,2:T(8,128)(2,1)} %reshape.344), slice={[0:32], [0:248], [0:2], [0:128]} | slice | bytes 8126464 | tf_op jit(solution)/shard_map/split | solution.py:52
  198.3 7.9 %copy.65 = bf16[32,248,2,128]{3,1,2,0:T(8,128)(2,1)} copy(bf16[32,248,2,128]{1,0,3,2:T(8,128)(2,1)} %split.8) | data formatting | bytes 8126464
  206.3 39.3 %reduce-scatter.9.cloned.1.call-done = bf16[4,260,2,128]{3,1,2,0:T(8,128)(2,1)} async-done(((bf16[32,260,2,128]{3,1,2,0:T(8,128)(2,1)}), bf16[4,260,2,128]{3,1,2,0:T(8,128)(2,1)}) %reduce-scatter.9.cloned.1.call-update) | async-done | bytes 532496 | tf_op jit(solution)/shard_map/reduce_scatter | solution.py:43
  245.7 49.5 %reduce-scatter.5.cloned.1.call-done = bf16[8,248,2,128]{3,1,2,0:T(8,128)(2,1)} async-done(((bf16[32,248,2,128]{3,1,2,0:T(8,128)(2,1)}), bf16[8,248,2,128]{3,1,2,0:T(8,128)(2,1)}) %reduce-scatter.5.cloned.1.call-update) | async-done | bytes 1015824 | tf_op jit(solution)/shard_map/reduce_scatter | solution.py:43
  295.2 0.6 broadcast_in_dim.23
  295.8 8.0 %all-to-all-start.2 = ((f32[32,1,128]{2,1,0:T(1,128)}), f32[32,1,128]{2,1,0:T(1,128)S(1)}, u32[]{:S(2)}, u32[]{:S(2)}) async-start(f32[32,1,128]{2,1,0:T(1,128)} %broadcast_in_dim.23), calls=%async_computation.6 | async-start | bytes 32768 | tf_op jit(solution)/shard_map/all_to_all | solution.py:16
  303.8 1.1 constant_dynamic-slice_fusion
  305.0 7.5 %all-to-all-done.2 = f32[32,1,128]{2,1,0:T(1,128)S(1)} async-done(((f32[32,1,128]{2,1,0:T(1,128)}), f32[32,1,128]{2,1,0:T(1,128)S(1)}, u32[]{:S(2)}, u32[]{:S(2)}) %all-to-all-start.2) | async-done | bytes 16416 | tf_op jit(solution)/shard_map/all_to_all | solution.py:16
  312.5 6.9 %reduce-scatter.11.cloned.1.call-done = bf16[1,260,2,128]{3,1,2,0:T(8,128)(2,1)} async-done(((bf16[4,260,2,128]{3,1,2,0:T(8,128)(2,1)}), bf16[1,260,2,128]{3,1,2,0:T(8,128)(2,1)}) %reduce-scatter.11.cloned.1.call-update) | async-done | bytes 133136 | tf_op jit(solution)/shard_map/reduce_scatter | solution.py:43
  319.4 38.5 %reduce-scatter.7.cloned.1.call-done = bf16[1,248,2,128]{3,1,2,0:T(8,128)(2,1)} async-done(((bf16[8,248,2,128]{3,1,2,0:T(8,128)(2,1)}), bf16[1,248,2,128]{3,1,2,0:T(8,128)(2,1)}) %reduce-scatter.7.cloned.1.call-update) | async-done | bytes 126992 | tf_op jit(solution)/shard_map/reduce_scatter | solution.py:43
  357.8 1.0 bitcast_subtract_fusion
  358.9 1.2 fusion.39
  360.1 0.4 fusion.12
  360.5 1.1 broadcast_in_dim.24
  361.6 9.9 %all-to-all-start.3 = ((bf16[8,64,2,508]{3,1,2,0:T(8,128)(2,1)}), bf16[8,64,2,508]{3,1,2,0:T(8,128)(2,1)S(1)}, u32[]{:S(2)}, u32[]{:S(2)}) async-start(bf16[8,64,2,508]{3,1,2,0:T(8,128)(2,1)} %broadcast_in_dim.24), calls=%async_computation.7 | async-start | bytes 2097152 | tf_op jit(solution)/shard_map/all_to_all | solution.py:16
  371.6 1.2 copy.59
  372.8 13.7 %all-to-all-done.3 = bf16[8,64,2,508]{3,1,2,0:T(8,128)(2,1)S(1)} async-done(((bf16[8,64,2,508]{3,1,2,0:T(8,128)(2,1)}), bf16[8,64,2,508]{3,1,2,0:T(8,128)(2,1)S(1)}, u32[]{:S(2)}, u32[]{:S(2)}) %all-to-all-start.3) | async-done | bytes 1040416 | tf_op jit(solution)/shard_map/all_to_all | solution.py:16
  386.6 0.9 copy.60
  (48 shorter events, 1.5 us)
Async XLA Ops:
  7.2 1.5 copy-start
  7.2 4.6 %copy-start.6 = (s32[1,512]{1,0:T(1,128)S(1)}, s32[1,512]{1,0:T(1,128)}, u32[]{:S(2)}) copy-start(s32[1,512]{1,0:T(1,128)} %param.10) | copy-start | bytes 6148
  7.2 4.7 %copy-start.8 = (s32[32]{0:T(128)S(1)}, s32[32]{0:T(128)}, u32[]{:S(2)}) copy-start(s32[32]{0:T(128)} %param.8) | copy-start | bytes 388
  7.2 4.7 %copy-start.2 = (bf16[32,2,16256]{2,1,0:T(2,128)(2,1)S(1)}, bf16[32,2,16256]{2,1,0:T(2,128)(2,1)}, u32[]{:S(2)}) copy-start(bf16[32,2,16256]{2,1,0:T(2,128)(2,1)} %param.7) | copy-start | bytes 6242308
  7.2 105.3 %all-gather.2.cloned.1.call-start = ((), (), s32[]{:S(2)}) async-start(), calls=%async_computation.8 | async-start | bytes 8583168 | tf_op jit(solution)/shard_map/all_gather | solution.py:103
  11.7 233.9 %reduce-scatter.9.cloned.1.call-start = ((), (), s32[]{:S(2)}) async-start(), calls=%async_computation.11 | async-start | bytes 4866048 | tf_op jit(solution)/shard_map/reduce_scatter | solution.py:43
  22.9 108.1 %copy-start.9 = (f32[32]{0:T(128)S(1)}, f32[32]{0:T(128)}, u32[]{:S(2)}) copy-start(f32[32]{0:T(128)} %param.9) | copy-start | bytes 388
  112.5 18.5 %copy-start.1 = (bf16[128,2,16256]{0,1,2:T(2,128)(2,1)S(1)}, bf16[128,2,16256]{0,1,2:T(2,128)(2,1)}, u32[]{:S(2)}) copy-start(bf16[128,2,16256]{0,1,2:T(2,128)(2,1)} %all-gather.2.cloned.1.call-done) | copy-start | bytes 24969220
  150.5 5.6 %copy-start.5 = (f32[32,128]{1,0:T(8,128)}, f32[32,128]{1,0:T(8,128)S(1)}, u32[]{:S(2)}) copy-start(f32[32,128]{1,0:T(8,128)S(1)} %get-tuple-element.19) | copy-start | bytes 49156
  193.6 101.5 %reduce-scatter.5.cloned.1.call-start = ((), (), s32[]{:S(2)}) async-start(), calls=%async_computation.9 | async-start | bytes 5079040 | tf_op jit(solution)/shard_map/reduce_scatter | solution.py:43
  206.2 152.7 %copy-start.7 = (f32[128]{0:T(128)S(1)}, f32[128]{0:T(128)}, u32[]{:S(2)}) copy-start(f32[128]{0:T(128)} %param.13) | copy-start | bytes 1540
  206.2 113.1 %reduce-scatter.11.cloned.1.call-start = ((), (), s32[]{:S(2)}) async-start(), calls=%async_computation.12 | async-start | bytes 675840 | tf_op jit(solution)/shard_map/reduce_scatter | solution.py:43
  245.6 112.2 %reduce-scatter.7.cloned.1.call-start = ((), (), s32[]{:S(2)}) async-start(), calls=%async_computation.10 | async-start | bytes 1142784 | tf_op jit(solution)/shard_map/reduce_scatter | solution.py:43
  295.8 16.6 %all-to-all-start.2 = ((f32[32,1,128]{2,1,0:T(1,128)}), f32[32,1,128]{2,1,0:T(1,128)S(1)}, u32[]{:S(2)}, u32[]{:S(2)}) async-start(f32[32,1,128]{2,1,0:T(1,128)} %broadcast_in_dim.23), calls=%async_computation.6 | async-start | bytes 32768 | tf_op jit(solution)/shard_map/all_to_all | solution.py:16
  360.1 11.4 %copy-start.3 = (bf16[1,260,2,128]{3,1,2,0:T(8,128)(2,1)S(1)}, bf16[1,260,2,128]{3,1,2,0:T(8,128)(2,1)}, u32[]{:S(2)}) copy-start(bf16[1,260,2,128]{3,1,2,0:T(8,128)(2,1)} %reduce-scatter.11.cloned.1.call-done) | copy-start | bytes 399364
  360.1 11.4 %copy-start.4 = (bf16[1,248,2,128]{3,1,2,0:T(8,128)(2,1)S(1)}, bf16[1,248,2,128]{3,1,2,0:T(8,128)(2,1)}, u32[]{:S(2)}) copy-start(bf16[1,248,2,128]{3,1,2,0:T(8,128)(2,1)} %reduce-scatter.7.cloned.1.call-done) | copy-start | bytes 380932
  361.6 24.8 %all-to-all-start.3 = ((bf16[8,64,2,508]{3,1,2,0:T(8,128)(2,1)}), bf16[8,64,2,508]{3,1,2,0:T(8,128)(2,1)S(1)}, u32[]{:S(2)}, u32[]{:S(2)}) async-start(bf16[8,64,2,508]{3,1,2,0:T(8,128)(2,1)} %broadcast_in_dim.24), calls=%async_computation.7 | async-start | bytes 2097152 | tf_op jit(solution)/shard_map/all_to_all | solution.py:16
Sparse Core Ops, SparseCore 0:
  11.8 100.6 all-gather.1
  193.8 51.7 reduce-scatter.8
  248.2 46.9 reduce-scatter.4
  297.6 21.7 reduce-scatter.10
  321.7 36.0 reduce-scatter.6
where the time goes:
time: 395 us; the launch traced here: 394 us
  waiting for transfers between devices  245 us (62%)
  local copies, waits for them, and re-layouts  60.2 us (15%)
  other arithmetic  31.3 us (8%)
  starting transfers between devices  18.1 us (5%)
  blocking collectives  17.7 us (4%)
  between operations  14.1 us (4%)
  matrix products  7.7 us (2%)
    reduce_scatter x4, waiting for transfers between devices, own_block(): tiles = lax.psum_scatter(tiles, axes[k], scatter_dimension=0, tiled=True)  134 us
    all_gather x1, waiting for transfers between devices, shards(): slices = lax.all_gather(own_part, IMG, axis=2, tiled=True)  89.6 us
    all_to_all x2, waiting for transfers between devices, sent_to_all(): lax.all_to_all(jnp.broadcast_to(x[None], (devices, *x.shape)), axis, 0, 0...  21.2 us
    reshape x1, local copies, waits for them, and re-layouts, split_up(): return jnp.moveaxis(x.reshape(*before, devices, -1, *after), dim, 0)  20.1 us
    reduce_sum x1, other arithmetic, shards(): energies = jnp.sum(jnp.square(slices.astype(jnp.float32)), axis=(1, 2))  18.5 us
    all_to_all x2, starting transfers between devices, sent_to_all(): lax.all_to_all(jnp.broadcast_to(x[None], (devices, *x.shape)), axis, 0, 0...  17.9 us
    all_to_all x2, blocking collectives, sent_to_all(): lax.all_to_all(jnp.broadcast_to(x[None], (devices, *x.shape)), axis, 0, 0...  17.7 us
    reshape x2, local copies, waits for them, and re-layouts, own_block(): tiles = tiles.reshape(*(lax.axis_size(a) for a in axes), *inside)  17.5 us
  transfers between devices with their start and end apart: 7, of which 7 were waited for; matrix products, arithmetic and copies ran while one was open for 7% of the time, Pallas kernels for 0%

commit v1 on v0

--- a/solution.py
+++ b/solution.py
@@ -100,7 +100,8 @@
     column_start = lax.axis_index(IMG) * part_width
     orient_ids = lax.axis_index("ori") * local_orients + jnp.arange(local_orients, dtype=jnp.int32)
     own_part = project_piece(volume, column_start, tilts, azimuth)
-    slices = lax.all_gather(own_part, IMG, axis=2, tiled=True)
+    stack = jnp.stack([own_part] * lax.axis_size(IMG))
+    slices = jnp.concatenate(lax.all_to_all(stack, IMG, 0, 0), axis=2)
     rotated = rotate_images(images, shifts)
     flat_images = rotated.reshape(image_count, 2 * full_width)
     flat_slices = slices.reshape(local_orients, 2 * full_width)

time: 395 us -> 543 us (1.37)
  waiting for transfers between devices: 245 us -> 339 us
  local copies, waits for them, and re-layouts: 60.2 us -> 96.5 us
  starting transfers between devices: 18.1 us -> 29.9 us
    all_to_all x0 -> x1, waiting for transfers between devices: none -> 173 us  [shards(): slices = jnp.concatenate(lax.all_to_all(stack, IMG, 0, 0), axis=2)]
    all_gather x1 -> x0, waiting for transfers between devices: 89.6 us -> none  [shards(): slices = lax.all_gather(own_part, IMG, axis=2, tiled=True)]
    another operation x0 -> x2, local copies, waits for them, and re-layouts: none -> 20.2 us  [the longest x1 14.6 us: shards(): flat_slices = slices.reshape(local_orients, 2 * full_width)]
    reshape x0 -> x1, local copies, waits for them, and re-layouts: none -> 15.4 us  [shards(): slices = jnp.concatenate(lax.all_to_all(stack, IMG, 0, 0), axis=2)]
    all_to_all x0 -> x1, starting transfers between devices: none -> 12.3 us  [shards(): slices = jnp.concatenate(lax.all_to_all(stack, IMG, 0, 0), axis=2)]
    reduce_scatter x4, waiting for transfers between devices: 134 us -> 144 us  [own_block(): tiles = lax.psum_scatter(tiles, axes[k], scatter_dimension=0, tiled=True)]
  transfers between devices with their start and end apart: 7 -> 7, of which waited for: 7 -> 7; matrix products, arithmetic and copies ran while one was open for 7% -> 5% of each run, Pallas kernels for 0% -> 0%
where the time goes in v1:
time: 543 us; the launch traced here: 541 us
  waiting for transfers between devices  339 us (62%)
  local copies, waits for them, and re-layouts  96.5 us (18%)
  other arithmetic  31.4 us (6%)
  starting transfers between devices  29.9 us (6%)
  blocking collectives  18 us (3%)
  between operations  14 us (3%)
  matrix products  13.1 us (2%)
    all_to_all x1, waiting for transfers between devices, shards(): slices = jnp.concatenate(lax.all_to_all(stack, IMG, 0, 0), axis=2)  173 us
    reduce_scatter x4, waiting for transfers between devices, own_block(): tiles = lax.psum_scatter(tiles, axes[k], scatter_dimension=0, tiled=True)  144 us
    all_to_all x2, waiting for transfers between devices, sent_to_all(): lax.all_to_all(jnp.broadcast_to(x[None], (devices, *x.shape)), axis, 0, 0...  21.2 us
    reshape x1, local copies, waits for them, and re-layouts, split_up(): return jnp.moveaxis(x.reshape(*before, devices, -1, *after), dim, 0)  20.1 us
    reduce_sum x1, other arithmetic, shards(): energies = jnp.sum(jnp.square(slices.astype(jnp.float32)), axis=(1, 2))  18.4 us
    all_to_all x2, blocking collectives, sent_to_all(): lax.all_to_all(jnp.broadcast_to(x[None], (devices, *x.shape)), axis, 0, 0...  18 us
    reshape x2, local copies, waits for them, and re-layouts, own_block(): tiles = tiles.reshape(*(lax.axis_size(a) for a in axes), *inside)  17.5 us
    all_to_all x2, starting transfers between devices, sent_to_all(): lax.all_to_all(jnp.broadcast_to(x[None], (devices, *x.shape)), axis, 0, 0...  17.5 us
  transfers between devices with their start and end apart: 7, of which 7 were waited for; matrix products, arithmetic and copies ran while one was open for 5% of the time, Pallas kernels for 0%

profile of v1, /device:TPU:1, one launch (start us, length us, event | category | flops | bytes accessed | tf_op | source)
XLA Modules:
  0.0 541.5 jit_solution(14305668239994969168)
XLA Ops:
  7.2 1.1 reshape.357
  8.7 1.8 fusion.29
  10.7 5.6 %stack.11 = bf16[32,128,2,508]{1,2,3,0:T(2,128)(2,1)} broadcast(bf16[128,2,508]{0,1,2:T(2,128)(2,1)S(1)} %copy.58), dimensions={1,2,3} | broadcast | bytes 8583168 | tf_op jit(solution)/shard_map/stack | solution.py:103
  16.3 12.3 %all-to-all-start = ((bf16[32,128,2,508]{1,2,3,0:T(2,128)(2,1)}), bf16[32,128,2,508]{1,2,3,0:T(2,128)(2,1)}, u32[]{:S(2)}, u32[]{:S(2)}) async-start(bf16[32,128,2,508]{1,2,3,0:T(2,128)(2,1)} %stack.11), calls=%async_computation | async-start | bytes 16646144 | tf_op jit(solution)/shard_map/all_to_all | solution.py:104
  28.7 3.0 fusion.52
  31.7 8.0 %fusion.6 = (bf16[32,1,16256]{2,0,1:T(8,128)(2,1)S(1)}, bf16[32,1,16256]{2,0,1:T(8,128)(2,1)S(1)}) fusion(f32[16256]{0:T(1024)S(1)} %fusion.35, f32[32]{0:T(128)S(1)} %convert_multiply_fusion, bf16[32,1,16256]{2,1,0:T(2,128)(2,1)S(1)} %get-tuple-element.23, bf16[32,1,16256]{2,1,0:T(2,128)(2,1)S(1)} %get-tuple-element.22), kind=kLoop, calls=%fused_computation.12 | loop fusion | flops 5722112 | bytes 4226688 | tf_op jit(solution)/shard_map/convert.2
  39.9 1.5 copy.80
  41.6 173.4 %all-to-all-done = bf16[32,128,2,508]{1,2,3,0:T(2,128)(2,1)} async-done(((bf16[32,128,2,508]{1,2,3,0:T(2,128)(2,1)}), bf16[32,128,2,508]{1,2,3,0:T(2,128)(2,1)}, u32[]{:S(2)}, u32[]{:S(2)}) %all-to-all-start) | async-done | bytes 8323104 | tf_op jit(solution)/shard_map/all_to_all | solution.py:104
  214.9 18.4 %multiply_reduce_fusion = f32[128]{0:T(128)S(1)} fusion(bf16[32,128,2,508]{1,2,3,0:T(2,128)(2,1)} %all-to-all-done), kind=kLoop, calls=%fused_computation.2 | loop fusion | flops 12484480 | bytes 8323584 | tf_op jit(solution)/shard_map/reduce_sum | solution.py:111
  233.3 15.4 %copy.59 = bf16[128,2,32,508]{3,2,1,0:T(8,128)(2,1)} copy(bf16[128,2,32,508]{0,1,3,2:T(2,128)(2,1)} %bitcast.3) | data formatting | bytes 16646144 | tf_op jit(solution)/shard_map/reshape | solution.py:104
  248.7 14.6 %reshape_reshape.3 = bf16[128,32512]{1,0:T(8,128)(2,1)} reshape(bf16[128,2,32,508]{3,2,1,0:T(8,128)(2,1)} %copy.59) | data formatting | bytes 16646144 | tf_op jit(solution)/shard_map/reshape;reshape | solution.py:107
  263.4 6.9 %fusion.53 = (f32[32]{0:T(128)S(1)}, f32[32,128]{1,0:T(8,128)S(1)}) fusion(f32[128]{0:T(128)S(1)} %broadcast_multiply_fusion, bf16[32,32512]{1,0:T(8,128)(2,1)} %bitcast.43, bf16[128,32512]{1,0:T(8,128)(2,1)} %reshape_reshape.3, f32[32]{0:T(128)S(1)} %copy-done.7, pred[128]{0:T(512)(128)(4,1)S(1)} %compare_reduce_fusion), kind=kOutput, calls=%fused_computation.79 | convolution fusion | flops 266358752 | bytes 10421120 | tf_op jit(solution)/shard_map/dot_general | solution.py:108
  270.3 10.2 %all_to_all.28 = f32[8,1,32]{2,1,0:T(1,128)S(1)} all-to-all(f32[8,1,32]{2,1,0:T(1,128)S(1)} %broadcast_in_dim.20), channel_id=1, replica_groups=mesh['img_0'=4,'img_1'=8,'ori'=8] {'ori'}, dimensions={0} | all-to-all | bytes 2048 | tf_op jit(solution)/shard_map/all_to_all | solution.py:16
  280.7 7.8 %all_to_all.29 = f32[8,1,32]{2,1,0:T(1,128)S(1)} all-to-all(f32[8,1,32]{2,1,0:T(1,128)S(1)} %broadcast_in_dim.22), channel_id=1, replica_groups=mesh['img_0'=4,'img_1'=8,'ori'=8] {'ori'}, dimensions={0} | all-to-all | bytes 2048 | tf_op jit(solution)/shard_map/all_to_all | solution.py:16
  288.6 5.5 %fusion = bf16[16256,2,128]{0,2,1:T(8,128)(2,1)} fusion(bf16[32,1,16256]{2,0,1:T(8,128)(2,1)S(1)} %get-tuple-element.21, bf16[32,1,16256]{2,0,1:T(8,128)(2,1)S(1)} %get-tuple-element.20, f32[32,128]{1,0:T(8,128)S(1)} %get-tuple-element.19), kind=kOutput, calls=%fused_computation.1 | convolution fusion | flops 274665472 | bytes 10420224 | tf_op jit(solution)/shard_map/ick,io->kco/dot_general | solution.py:124
  294.2 20.1 %reshape.365 = bf16[32,508,2,128]{1,0,3,2:T(8,128)(2,1)} reshape(bf16[16256,2,128]{0,2,1:T(8,128)(2,1)} %fusion) | data formatting | bytes 16646144 | tf_op jit(solution)/shard_map/reshape | solution.py:30
  314.3 9.1 %slice_bitcast_fusion = bf16[4,8,260,2,128]{2,1,0,4,3:T(8,128)(2,1)} fusion(bf16[32,508,2,128]{1,0,3,2:T(8,128)(2,1)} %reshape.365), kind=kLoop, calls=%fused_computation.3 | loop fusion | bytes 8519680 | tf_op jit(solution)/shard_map/reshape | solution.py:40
  323.3 8.4 %copy.64 = bf16[4,8,260,2,128]{4,2,3,0,1:T(8,128)(2,1)} copy(bf16[4,8,260,2,128]{2,1,0,4,3:T(8,128)(2,1)} %slice_bitcast_fusion) | data formatting | bytes 8519680 | tf_op jit(solution)/shard_map/reshape | solution.py:40
  331.8 4.6 split.8
  336.4 7.9 %copy.76 = bf16[32,248,2,128]{3,1,2,0:T(8,128)(2,1)} copy(bf16[32,248,2,128]{1,0,3,2:T(8,128)(2,1)} %split.8) | data formatting | bytes 8126464
  344.4 48.5 %reduce-scatter.9.cloned.1.call-done = bf16[4,260,2,128]{3,1,2,0:T(8,128)(2,1)} async-done(((bf16[32,260,2,128]{3,1,2,0:T(8,128)(2,1)}), bf16[4,260,2,128]{3,1,2,0:T(8,128)(2,1)}) %reduce-scatter.9.cloned.1.call-update) | async-done | bytes 532496 | tf_op jit(solution)/shard_map/reduce_scatter | solution.py:43
  392.9 49.5 %reduce-scatter.5.cloned.1.call-done = bf16[8,248,2,128]{3,1,2,0:T(8,128)(2,1)} async-done(((bf16[32,248,2,128]{3,1,2,0:T(8,128)(2,1)}), bf16[8,248,2,128]{3,1,2,0:T(8,128)(2,1)}) %reduce-scatter.5.cloned.1.call-update) | async-done | bytes 1015824 | tf_op jit(solution)/shard_map/reduce_scatter | solution.py:43
  443.0 8.0 %all-to-all-start.3 = ((f32[32,1,128]{2,1,0:T(1,128)}), f32[32,1,128]{2,1,0:T(1,128)S(1)}, u32[]{:S(2)}, u32[]{:S(2)}) async-start(f32[32,1,128]{2,1,0:T(1,128)} %broadcast_in_dim.23), calls=%async_computation.7 | async-start | bytes 32768 | tf_op jit(solution)/shard_map/all_to_all | solution.py:16
  451.0 1.1 constant_dynamic-slice_fusion
  452.2 7.5 %all-to-all-done.3 = f32[32,1,128]{2,1,0:T(1,128)S(1)} async-done(((f32[32,1,128]{2,1,0:T(1,128)}), f32[32,1,128]{2,1,0:T(1,128)S(1)}, u32[]{:S(2)}, u32[]{:S(2)}) %all-to-all-start.3) | async-done | bytes 16416 | tf_op jit(solution)/shard_map/all_to_all | solution.py:16
  459.7 7.1 %reduce-scatter.11.cloned.1.call-done = bf16[1,260,2,128]{3,1,2,0:T(8,128)(2,1)} async-done(((bf16[4,260,2,128]{3,1,2,0:T(8,128)(2,1)}), bf16[1,260,2,128]{3,1,2,0:T(8,128)(2,1)}) %reduce-scatter.11.cloned.1.call-update) | async-done | bytes 133136 | tf_op jit(solution)/shard_map/reduce_scatter | solution.py:43
  466.7 39.0 %reduce-scatter.7.cloned.1.call-done = bf16[1,248,2,128]{3,1,2,0:T(8,128)(2,1)} async-done(((bf16[8,248,2,128]{3,1,2,0:T(8,128)(2,1)}), bf16[1,248,2,128]{3,1,2,0:T(8,128)(2,1)}) %reduce-scatter.7.cloned.1.call-update) | async-done | bytes 126992 | tf_op jit(solution)/shard_map/reduce_scatter | solution.py:43
  506.7 1.2 fusion.26
  508.4 1.1 broadcast_in_dim.24
  509.5 9.4 %all-to-all-start.4 = ((bf16[8,64,2,508]{3,1,2,0:T(8,128)(2,1)}), bf16[8,64,2,508]{3,1,2,0:T(8,128)(2,1)S(1)}, u32[]{:S(2)}, u32[]{:S(2)}) async-start(bf16[8,64,2,508]{3,1,2,0:T(8,128)(2,1)} %broadcast_in_dim.24), calls=%async_computation.8 | async-start | bytes 2097152 | tf_op jit(solution)/shard_map/all_to_all | solution.py:16
  519.0 1.2 copy.68
  520.2 13.7 %all-to-all-done.4 = bf16[8,64,2,508]{3,1,2,0:T(8,128)(2,1)S(1)} async-done(((bf16[8,64,2,508]{3,1,2,0:T(8,128)(2,1)}), bf16[8,64,2,508]{3,1,2,0:T(8,128)(2,1)S(1)}, u32[]{:S(2)}, u32[]{:S(2)}) %all-to-all-start.4) | async-done | bytes 1040416 | tf_op jit(solution)/shard_map/all_to_all | solution.py:16
  (50 shorter events, 4.8 us)
Async XLA Ops:
  7.2 1.3 copy-start
  16.3 12.3 %copy-start.8 = (s32[32]{0:T(128)S(1)}, s32[32]{0:T(128)}, u32[]{:S(2)}) copy-start(s32[32]{0:T(128)} %param.8) | copy-start | bytes 388
  16.3 12.4 %copy-start.1 = (bf16[32,2,16256]{2,1,0:T(2,128)(2,1)S(1)}, bf16[32,2,16256]{2,1,0:T(2,128)(2,1)}, u32[]{:S(2)}) copy-start(bf16[32,2,16256]{2,1,0:T(2,128)(2,1)} %param.7) | copy-start | bytes 6242308
  16.3 198.6 %all-to-all-start = ((bf16[32,128,2,508]{1,2,3,0:T(2,128)(2,1)}), bf16[32,128,2,508]{1,2,3,0:T(2,128)(2,1)}, u32[]{:S(2)}, u32[]{:S(2)}) async-start(bf16[32,128,2,508]{1,2,3,0:T(2,128)(2,1)} %stack.11), calls=%async_computation | async-start | bytes 16646144 | tf_op jit(solution)/shard_map/all_to_all | solution.py:104
  28.6 364.2 %reduce-scatter.9.cloned.1.call-start = ((), (), s32[]{:S(2)}) async-start(), calls=%async_computation.11 | async-start | bytes 4866048 | tf_op jit(solution)/shard_map/reduce_scatter | solution.py:43
  39.9 1.5 copy-start.5
  248.7 14.6 %copy-start.7 = (f32[32]{0:T(128)S(1)}, f32[32]{0:T(128)}, u32[]{:S(2)}) copy-start(f32[32]{0:T(128)} %param.9) | copy-start | bytes 388
  288.6 5.6 %copy-start.4 = (f32[32,128]{1,0:T(8,128)}, f32[32,128]{1,0:T(8,128)S(1)}, u32[]{:S(2)}) copy-start(f32[32,128]{1,0:T(8,128)S(1)} %get-tuple-element.19) | copy-start | bytes 49156
  331.7 110.6 %reduce-scatter.5.cloned.1.call-start = ((), (), s32[]{:S(2)}) async-start(), calls=%async_computation.9 | async-start | bytes 5079040 | tf_op jit(solution)/shard_map/reduce_scatter | solution.py:43
  344.3 162.4 %copy-start.6 = (f32[128]{0:T(128)S(1)}, f32[128]{0:T(128)}, u32[]{:S(2)}) copy-start(f32[128]{0:T(128)} %param.13) | copy-start | bytes 1540
  344.3 122.4 %reduce-scatter.11.cloned.1.call-start = ((), (), s32[]{:S(2)}) async-start(), calls=%async_computation.12 | async-start | bytes 675840 | tf_op jit(solution)/shard_map/reduce_scatter | solution.py:43
  392.8 112.9 %reduce-scatter.7.cloned.1.call-start = ((), (), s32[]{:S(2)}) async-start(), calls=%async_computation.10 | async-start | bytes 1142784 | tf_op jit(solution)/shard_map/reduce_scatter | solution.py:43
  443.0 16.6 %all-to-all-start.3 = ((f32[32,1,128]{2,1,0:T(1,128)}), f32[32,1,128]{2,1,0:T(1,128)S(1)}, u32[]{:S(2)}, u32[]{:S(2)}) async-start(f32[32,1,128]{2,1,0:T(1,128)} %broadcast_in_dim.23), calls=%async_computation.7 | async-start | bytes 32768 | tf_op jit(solution)/shard_map/all_to_all | solution.py:16
  507.9 11.0 %copy-start.2 = (bf16[1,260,2,128]{3,1,2,0:T(8,128)(2,1)S(1)}, bf16[1,260,2,128]{3,1,2,0:T(8,128)(2,1)}, u32[]{:S(2)}) copy-start(bf16[1,260,2,128]{3,1,2,0:T(8,128)(2,1)} %reduce-scatter.11.cloned.1.call-done) | copy-start | bytes 399364
  507.9 11.0 %copy-start.3 = (bf16[1,248,2,128]{3,1,2,0:T(8,128)(2,1)S(1)}, bf16[1,248,2,128]{3,1,2,0:T(8,128)(2,1)}, u32[]{:S(2)}) copy-start(bf16[1,248,2,128]{3,1,2,0:T(8,128)(2,1)} %reduce-scatter.7.cloned.1.call-done) | copy-start | bytes 380932
  509.5 24.4 %all-to-all-start.4 = ((bf16[8,64,2,508]{3,1,2,0:T(8,128)(2,1)}), bf16[8,64,2,508]{3,1,2,0:T(8,128)(2,1)S(1)}, u32[]{:S(2)}, u32[]{:S(2)}) async-start(bf16[8,64,2,508]{3,1,2,0:T(8,128)(2,1)} %broadcast_in_dim.24), calls=%async_computation.8 | async-start | bytes 2097152 | tf_op jit(solution)/shard_map/all_to_all | solution.py:16
Sparse Core Ops, SparseCore 0:
  331.9 60.9 reduce-scatter.8
  395.4 46.9 reduce-scatter.4
  444.9 21.7 reduce-scatter.10
  469.1 36.5 reduce-scatter.6
